TPU v7x, 32 devices: a whole 2x2x4 slice. The times are simulated.
32 devices in a mesh: seq: 2 (over core), head: 4 (over y, x), batch: 4 (over z).
Axes of the slice: x: 2, y: 2, z: 4, core: 2. Of those that a mesh axis runs over, the one named last changes fastest.
Arguments:
- block_in: bfloat16 [4, 1024, 768], P('batch', 'seq'), may hold values from -6 to 6
- out_grad: bfloat16 [4, 1024, 768], P('batch', 'seq'), may hold values from -6 to 6
- norm_gain: float32 [768], replicated, may hold values from 0.5 to 1.5
- in_proj: float32 [2, 768, 1536], P(None, ('seq', 'batch'), 'head'), may hold values from -0.21875 to 0.21875
- bc_proj: float32 [768, 256], P('head', ('seq', 'batch')), may hold values from -0.21875 to 0.21875
- dt_proj: float32 [768, 24], P(('seq', 'batch'), 'head'), may hold values from -0.21875 to 0.21875
- out_proj: float32 [1536, 768], P('head', ('seq', 'batch')), may hold values from -0.15625 to 0.15625
- chan_params: float32 [6, 1536], P(None, 'head'), may hold values from -0.6 to 1.5, as said below
- head_params: float32 [3, 24], P(None, 'head'), may hold values from -10 to 1.5, as said below
- bc_conv: float32 [5, 256], replicated, may hold values from -0.6 to 0.6, as said below
- first_norm_gain: float32 [768], replicated, may hold values from -60 to 60
- second_norm_gain: float32 [768], replicated, may hold values from 100 to 2000
- first_in_proj: float32 [2, 768, 1536], P(None, ('seq', 'batch'), 'head'), may hold values from -60 to 60
- second_in_proj: float32 [2, 768, 1536], P(None, ('seq', 'batch'), 'head'), may hold values from 100 to 2000
- first_bc_proj: float32 [768, 256], P('head', ('seq', 'batch')), may hold values from -60 to 60
- second_bc_proj: float32 [768, 256], P('head', ('seq', 'batch')), may hold values from 100 to 2000
- first_dt_proj: float32 [768, 24], P(('seq', 'batch'), 'head'), may hold values from -60 to 60
- second_dt_proj: float32 [768, 24], P(('seq', 'batch'), 'head'), may hold values from 100 to 2000
- first_out_proj: float32 [1536, 768], P('head', ('seq', 'batch')), may hold values from -60 to 60
- second_out_proj: float32 [1536, 768], P('head', ('seq', 'batch')), may hold values from 100 to 2000
- first_chan_params: float32 [6, 1536], P(None, 'head'), may hold values from -60 to 60
- second_chan_params: float32 [6, 1536], P(None, 'head'), may hold values from 100 to 2000
- first_head_params: float32 [3, 24], P(None, 'head'), may hold values from -60 to 60
- second_head_params: float32 [3, 24], P(None, 'head'), may hold values from 100 to 2000
- first_bc_conv: float32 [5, 256], replicated, may hold values from -60 to 60
- second_bc_conv: float32 [5, 256], replicated, may hold values from 100 to 2000
Outputs:
- block_out: bfloat16 [4, 1024, 768], P('batch', 'seq')
- in_grad: float32 [4, 1024, 768], P('batch', 'seq')
- grad_norm_gain: float32 [768], replicated
- grad_in_proj: float32 [2, 768, 1536], P(None, ('seq', 'batch'), 'head')
- grad_bc_proj: float32 [768, 256], P('head', ('seq', 'batch'))
- grad_dt_proj: float32 [768, 24], P(('seq', 'batch'), 'head')
- grad_out_proj: float32 [1536, 768], P('head', ('seq', 'batch'))
- grad_chan_params: float32 [6, 1536], P(None, 'head')
- grad_head_params: float32 [3, 24], P(None, 'head')
- grad_bc_conv: float32 [5, 256], replicated
- new_norm_gain: float32 [768], replicated
- new_in_proj: float32 [2, 768, 1536], P(None, ('seq', 'batch'), 'head')
- new_bc_proj: float32 [768, 256], P('head', ('seq', 'batch'))
- new_dt_proj: float32 [768, 24], P(('seq', 'batch'), 'head')
- new_out_proj: float32 [1536, 768], P('head', ('seq', 'batch'))
- new_chan_params: float32 [6, 1536], P(None, 'head')
- new_head_params: float32 [3, 24], P(None, 'head')
- new_bc_conv: float32 [5, 256], replicated
- new_first_norm_gain: float32 [768], replicated
- new_second_norm_gain: float32 [768], replicated
- new_first_in_proj: float32 [2, 768, 1536], P(None, ('seq', 'batch'), 'head')
- new_second_in_proj: float32 [2, 768, 1536], P(None, ('seq', 'batch'), 'head')
- new_first_bc_proj: float32 [768, 256], P('head', ('seq', 'batch'))
- new_second_bc_proj: float32 [768, 256], P('head', ('seq', 'batch'))
- new_first_dt_proj: float32 [768, 24], P(('seq', 'batch'), 'head')
- new_second_dt_proj: float32 [768, 24], P(('seq', 'batch'), 'head')
- new_first_out_proj: float32 [1536, 768], P('head', ('seq', 'batch'))
- new_second_out_proj: float32 [1536, 768], P('head', ('seq', 'batch'))
- new_first_chan_params: float32 [6, 1536], P(None, 'head')
- new_second_chan_params: float32 [6, 1536], P(None, 'head')
- new_first_head_params: float32 [3, 24], P(None, 'head')
- new_second_head_params: float32 [3, 24], P(None, 'head')
- new_first_bc_conv: float32 [5, 256], replicated
- new_second_bc_conv: float32 [5, 256], replicated
Inputs may be any that keep to these rules, and one draw needn't show every extreme that they name: `head_params`: row 0 holds the time-step biases, row 1 the logarithms of the decay rates, row 2 the skip gains. `chan_params`: rows 0 to 3 hold the taps, row 4 the bias, row 5 the gated-norm gain. `bc_conv`: rows 0 to 3 hold the taps, row 4 the bias.
All inputs are finite; a program needn't handle non-finite values.
Results may differ from a plain program's by a relative error of at most 0.012.
The roundings to bfloat16 on the way count: a program that leaves them out, or rounds other values in their place, can miss the bound.
Values may be sent and summed in bfloat16 or wider, within the bound.
A program may use at most 128 MiB of HBM per device.

v0:
```python
import jax
import jax.numpy as jnp
from jax import lax
from jax.experimental import pallas as pl
from jax.experimental.pallas import tpu as pltpu
from jax.sharding import PartitionSpec as P

D = 768
P_SIZE = 64
N = 128
K = 4
Q = 256
DI = 1536


eps_norm = 1e-05
beta_one = 0.9
beta_two = 0.95
adam_eps = 1e-08
rate_matrix = 0.01
rate_vector = 0.1
decay_matrix = 0.1
adam_step = 3.0
highest = lax.Precision.HIGHEST


def shifted(value, axis, steps):
    count = lax.axis_size(axis)
    leading, last = (max(0, -steps), min(count, count - steps))
    return lax.ppermute(value, axis, [(source, source + steps) for source in range(leading, last)])


def prefix(part, axis, combine, identity, reverse):
    count = lax.axis_size(axis)
    place = lax.axis_index(axis)
    ahead = count - 1 - place if reverse else place
    gathered = jax.tree.map(lambda a: lax.all_gather(a, axis), part)
    state = jax.tree.map(lambda a, e: jnp.zeros_like(a) + jnp.asarray(e, a.dtype), part, identity)

    def one(lap, state):
        source = count - 1 - lap if reverse else lap
        return combine(
            state, jax.tree.map(lambda a: lax.dynamic_index_in_dim(a, source, 0, False), gathered)
        )

    return lax.fori_loop(0, ahead, one, state)


def silu_grad(values):
    sigmoid_v = jax.nn.sigmoid(values)
    return sigmoid_v * (1.0 + values * (1.0 - sigmoid_v))


def dot_first(left_op, right_op):
    return lax.dot_general(
        left_op, right_op, (((0,), (0,)), ((), ())), preferred_element_type=jnp.float32
    )


def dot_last(left_op, right_op):
    return lax.dot_general(
        left_op, right_op, (((1,), (1,)), ((), ())), preferred_element_type=jnp.float32
    )


def dot_plain(left_op, right_op, contract):
    return lax.dot_general(
        left_op, right_op, ((contract[:1], contract[1:]), ((), ())),
        precision=highest, preferred_element_type=jnp.float32,
    )


def row_spans(tokens):
    size = Q if tokens % Q == 0 else tokens
    return [(start, size) for start in range(0, tokens, size)]


def causal_decay(cum_col, cum_row, start):
    shape = (cum_col.shape[0], cum_row.shape[1])
    rows = lax.broadcasted_iota(jnp.int32, shape, 0) + start
    cols = lax.broadcasted_iota(jnp.int32, shape, 1)
    return jnp.exp(jnp.where(rows >= cols, cum_col - cum_row, -jnp.inf))


def half_select(values, lane):
    return jnp.where(lane < P_SIZE, values[:, 0:1], values[:, 1:2])


def forward_kernel(x_ref, b_ref, c_ref, cols_ref, rows_ref, y_ref, state_ref, scores):
    tokens = x_ref.shape[0]
    spans = row_spans(tokens)

    @pl.when(pl.program_id(0) == 0)
    def _():
        for start, size in spans:
            scores[start : start + size, :] = dot_plain(
                c_ref[start : start + size, :], b_ref[...], (1, 1)
            )

    cols = cols_ref[0]
    rows = rows_ref[0]
    for start, size in spans:
        width = start + size
        lane = lax.broadcasted_iota(jnp.int32, (size, x_ref.shape[1]), 1)
        outs = []
        for head in range(2):
            decay = causal_decay(
                cols[start:width, head : head + 1], rows[head : head + 1, :width], start
            )
            mixing = scores[start:width, :width] * decay * rows[2 + head : 3 + head, :width]
            outs.append(dot_plain(mixing, x_ref[:width, :], (1, 0)))
        y_ref[start:width, :] = jnp.where(lane < P_SIZE, outs[0], outs[1])
    lane = lax.broadcasted_iota(jnp.int32, x_ref.shape, 1)
    weight = jnp.exp(cols[tokens - 1 :, :2] - cols[:, :2]) * cols[:, 2:]
    state_ref[...] = dot_plain(x_ref[...] * half_select(weight, lane), b_ref[...], (0, 0))


def backward_kernel(
    x_ref, b_ref, c_ref, cols_ref, rows_ref, dy_ref, state_ref, dstate_ref,
    dx_ref, db_ref, dc_ref, dcols_ref, drows_ref, scores, dscores, dx_acc,
):
    tokens = x_ref.shape[0]
    spans = row_spans(tokens)
    last = pl.program_id(0) == pl.num_programs(0) - 1

    @pl.when(pl.program_id(0) == 0)
    def _():
        for start, size in spans:
            scores[start : start + size, :] = dot_plain(
                c_ref[start : start + size, :], b_ref[...], (1, 1)
            )
        dscores[...] = jnp.zeros_like(dscores)
        db_ref[...] = jnp.zeros_like(db_ref)
        dc_ref[...] = jnp.zeros_like(dc_ref)

    cols = cols_ref[0]
    rows = rows_ref[0]
    lane = lax.broadcasted_iota(jnp.int32, x_ref.shape, 1)
    grow = jnp.exp(cols[:, :2])
    rest = jnp.exp(cols[tokens - 1 :, :2] - cols[:, :2])
    weight = rest * cols[:, 2:]
    x_all = x_ref[...]
    dy_all = dy_ref[...]
    weight_lane = half_select(weight, lane)
    dc_ref[...] += dot_plain(dy_all * half_select(grow, lane), state_ref[...], (1, 0))
    db_ref[...] += dot_plain(x_all * weight_lane, dstate_ref[...], (1, 0))
    from_state = dy_all * dot_plain(c_ref[...], state_ref[...], (1, 1))
    from_end = dot_plain(b_ref[...], dstate_ref[...], (1, 1))
    dx_acc[...] = from_end * weight_lane
    to_end = x_all * from_end
    pair_state = dstate_ref[...] * state_ref[...]
    last_row = lax.broadcasted_iota(jnp.int32, (tokens, 1), 0) == tokens - 1
    for head in range(2):
        mine = (lane < P_SIZE) if head == 0 else (lane >= P_SIZE)
        in_sum = jnp.sum(jnp.where(mine, from_state, 0.0), axis=1, keepdims=True)
        end_sum = jnp.sum(jnp.where(mine, to_end, 0.0), axis=1, keepdims=True)
        spent = weight[:, head : head + 1] * end_sum
        half = pair_state[head * P_SIZE : (head + 1) * P_SIZE, :]
        total = jnp.sum(spent, keepdims=True) + grow[tokens - 1 :, head : head + 1] * jnp.sum(
            half, keepdims=True
        )
        dcum = grow[:, head : head + 1] * in_sum - spent + jnp.where(last_row, total, 0.0)
        dcols_ref[0, :, head : head + 1] = dcum
        dcols_ref[0, :, 2 + head : 3 + head] = rest[:, head : head + 1] * end_sum
        dy_mine = jnp.where(mine, dy_all, 0.0)
        drows_ref[0, head : head + 1, :] = jnp.zeros((1, tokens), jnp.float32)
        for start, size in spans:
            width = start + size
            dt_row = rows[2 + head : 3 + head, :width]
            decay = causal_decay(
                cols[start:width, head : head + 1], rows[head : head + 1, :width], start
            )
            weighted = decay * dt_row
            dmix = dot_plain(dy_mine[start:width, :], x_all[:width, :], (1, 1))
            dscores[start:width, :width] += dmix * weighted
            mixing = scores[start:width, :width] * weighted
            dx_acc[:width, :] += dot_plain(mixing, dy_mine[start:width, :], (0, 0))
            dcols_ref[0, start:width, head : head + 1] += jnp.sum(
                dmix * mixing, axis=1, keepdims=True
            )
            drows_ref[0, head : head + 1, :width] += jnp.sum(
                dmix * decay * scores[start:width, :width], axis=0, keepdims=True
            )
    dx_ref[...] = dx_acc[...]

    @pl.when(last)
    def _():
        for start, size in spans:
            width = start + size
            dc_ref[start:width, :] += dot_plain(
                dscores[start:width, :width], b_ref[:width, :], (1, 0)
            )
            db_ref[:width, :] += dot_plain(
                dscores[start:width, :width], c_ref[start:width, :], (0, 0)
            )


def common_specs(tokens, pairs):
    wide = 2 * P_SIZE
    return [
        pl.BlockSpec((tokens, wide), lambda i: (0, i)),
        pl.BlockSpec((tokens, N), lambda i: (0, pairs)),
        pl.BlockSpec((tokens, N), lambda i: (0, pairs + 1)),
        pl.BlockSpec((1, tokens, 4), lambda i: (i, 0, 0)),
        pl.BlockSpec((1, 4, tokens), lambda i: (i, 0, 0)),
    ]


def ssd_forward(conv_all, cols, rows):
    tokens = conv_all.shape[0]
    pairs = cols.shape[0]
    wide = 2 * P_SIZE
    return pl.pallas_call(
        forward_kernel,
        grid=(pairs,),
        in_specs=common_specs(tokens, pairs),
        out_specs=[
            pl.BlockSpec((tokens, wide), lambda i: (0, i)),
            pl.BlockSpec((wide, N), lambda i: (i, 0)),
        ],
        out_shape=[
            jax.ShapeDtypeStruct((tokens, pairs * wide), jnp.float32),
            jax.ShapeDtypeStruct((pairs * wide, N), jnp.float32),
        ],
        scratch_shapes=[pltpu.VMEM((tokens, tokens), jnp.float32)],
        compiler_params=pltpu.CompilerParams(vmem_limit_bytes=32 << 20),
    )(conv_all, conv_all, conv_all, cols, rows)


def ssd_backward(conv_all, cols, rows, grad_ssd, state_in, grad_end):
    tokens = conv_all.shape[0]
    pairs = cols.shape[0]
    wide = 2 * P_SIZE
    pair_block = pl.BlockSpec((tokens, wide), lambda i: (0, i))
    state_block = pl.BlockSpec((wide, N), lambda i: (i, 0))
    shared_block = pl.BlockSpec((tokens, N), lambda i: (0, 0))
    return pl.pallas_call(
        backward_kernel,
        grid=(pairs,),
        in_specs=common_specs(tokens, pairs) + [pair_block, state_block, state_block],
        out_specs=[
            pair_block,
            shared_block,
            shared_block,
            pl.BlockSpec((1, tokens, 4), lambda i: (i, 0, 0)),
            pl.BlockSpec((1, 2, tokens), lambda i: (i, 0, 0)),
        ],
        out_shape=[
            jax.ShapeDtypeStruct((tokens, pairs * wide), jnp.float32),
            jax.ShapeDtypeStruct((tokens, N), jnp.float32),
            jax.ShapeDtypeStruct((tokens, N), jnp.float32),
            jax.ShapeDtypeStruct((pairs, tokens, 4), jnp.float32),
            jax.ShapeDtypeStruct((pairs, 2, tokens), jnp.float32),
        ],
        scratch_shapes=[
            pltpu.VMEM((tokens, tokens), jnp.float32),
            pltpu.VMEM((tokens, tokens), jnp.float32),
            pltpu.VMEM((tokens, wide), jnp.float32),
        ],
        compiler_params=pltpu.CompilerParams(vmem_limit_bytes=32 << 20),
    )(conv_all, conv_all, conv_all, cols, rows, grad_ssd, state_in, grad_end)


def combine_states(earlier, later):
    return (earlier[0] + later[0], jnp.exp(later[0])[:, None] * earlier[1] + later[1])


def adamw(weight, grad_sum, moment_one, moment_two, step_rate, decay_rate):
    first_new = beta_one * moment_one + (1.0 - beta_one) * grad_sum
    second_new = beta_two * moment_two + (1.0 - beta_two) * grad_sum * grad_sum
    first_hat = first_new / (1.0 - beta_one**adam_step)
    second_hat = second_new / (1.0 - beta_two**adam_step)
    updated = weight - step_rate * (
        first_hat / (jnp.sqrt(second_hat) + adam_eps) + decay_rate * weight
    )
    return (updated, first_new, second_new)


def per_device(
    block_in,
    out_grad,
    norm_gain,
    in_proj,
    bc_proj,
    dt_proj,
    out_proj,
    chan_params,
    head_params,
    bc_conv,
    first_norm_gain,
    second_norm_gain,
    first_in_proj,
    second_in_proj,
    first_bc_proj,
    second_bc_proj,
    first_dt_proj,
    second_dt_proj,
    first_out_proj,
    second_out_proj,
    first_chan_params,
    second_chan_params,
    first_head_params,
    second_head_params,
    first_bc_conv,
    second_bc_conv,
):
    shards = ("seq", "batch")
    block_rows = block_in[0]
    grad_rows = out_grad[0]
    tokens = block_rows.shape[0]
    head_local = head_params.shape[1]
    inner_local = chan_params.shape[1]
    shard_rows = in_proj.shape[1]
    pairs = head_local // 2
    edge_rows = K - 1
    half = jnp.bfloat16
    bc_heads = lax.all_gather(bc_proj.astype(half), "head", axis=0, tiled=True)
    spare = -head_local % 128
    packed = jnp.concatenate(
        [
            in_proj[0].astype(half),
            in_proj[1].astype(half),
            out_proj.astype(half).T,
            jnp.pad(dt_proj.astype(half), ((0, 0), (0, spare))),
            bc_heads.T.reshape(shard_rows, 2 * N),
        ],
        1,
    )
    full = lax.all_gather(packed, shards, axis=0, tiled=True)
    zx_full = full[:, : 2 * inner_local]
    out_t = full[:, 2 * inner_local : 3 * inner_local]
    dt_full = full[:, 3 * inner_local : 3 * inner_local + head_local]
    bc_t = full[:, 3 * inner_local + head_local + spare :].reshape(2 * N, D)
    block_f = block_rows.astype(jnp.float32)
    scaling_in = lax.rsqrt(jnp.mean(block_f * block_f, axis=-1, keepdims=True) + eps_norm)
    normed_b = (block_f * scaling_in * norm_gain[None, :]).astype(half)
    both_pre = jnp.dot(normed_b, zx_full, preferred_element_type=jnp.float32)
    gate_pre = both_pre[:, :inner_local]
    step_raw = jnp.dot(normed_b, dt_full, preferred_element_type=jnp.float32)
    conv_pre = jnp.concatenate([both_pre[:, inner_local:], dot_last(normed_b, bc_t)], 1)
    edge_in = shifted(conv_pre[tokens - edge_rows :], "seq", 1)
    padded = jnp.concatenate([edge_in, conv_pre], 0)
    taps = jnp.concatenate([chan_params[: K + 1], bc_conv], 1)
    summed = taps[K][None, :] + sum(
        taps[k][None, :] * padded[k : k + tokens] for k in range(K)
    )
    conv_all = jax.nn.silu(summed)
    inner_x = conv_all[:, :inner_local]
    c_rows = conv_all[:, inner_local + N :]
    steps_dt = jax.nn.softplus(step_raw + head_params[0][None, :])
    steps_log = -jnp.exp(head_params[1])[None, :] * steps_dt
    order = jnp.arange(tokens)
    lower = (order[:, None] >= order[None, :]).astype(jnp.float32)
    cumulative = jnp.dot(lower, steps_log, precision=highest)
    spread = (
        jnp.arange(head_local)[:, None] == jnp.arange(inner_local)[None, :] // P_SIZE
    ).astype(jnp.float32)
    decay_lane = jnp.dot(jnp.exp(cumulative), spread, precision=highest)
    rows = jnp.concatenate(
        [cumulative.T.reshape(pairs, 2, tokens), steps_dt.T.reshape(pairs, 2, tokens)], 1
    )
    cols = rows.transpose(0, 2, 1)
    local_out, local_state = ssd_forward(conv_all, cols, rows)
    device_log = jnp.repeat(cumulative[-1], P_SIZE)
    zero_log = jnp.zeros(device_log.shape, jnp.float32)
    zero_state = jnp.zeros(local_state.shape, jnp.float32)
    state_in = prefix(
        (device_log, local_state), "seq", combine_states, (zero_log, zero_state), False
    )[1]
    ssd_out = local_out + decay_lane * lax.dot_general(
        c_rows, state_in, (((1,), (1,)), ((), ())), precision=highest
    )
    skip_lane = jnp.repeat(head_params[2], P_SIZE)[None, :]
    mixed_rows = ssd_out + skip_lane * inner_x
    gate_act = jax.nn.silu(gate_pre)
    gated_rows = mixed_rows * gate_act
    gate_gain = chan_params[K + 1]
    grad_mixed = jnp.dot(grad_rows, out_t, preferred_element_type=jnp.float32)
    gain_grad = grad_mixed * gate_gain[None, :]
    square_sum, cross_sum = lax.psum(
        jnp.stack([jnp.sum(gated_rows * gated_rows, -1), jnp.sum(gain_grad * gated_rows, -1)]),
        "head",
    )
    scaling_gate = lax.rsqrt(square_sum / DI + eps_norm)[:, None]
    mixed_b = (gated_rows * scaling_gate * gate_gain[None, :]).astype(half)
    out_partial = dot_last(mixed_b, out_t)
    out_sum = lax.psum(out_partial.astype(half), "head")
    g_out_t = lax.psum_scatter(
        dot_first(grad_rows, mixed_b), shards, scatter_dimension=0, tiled=True
    )
    grad_f = grad_rows.astype(jnp.float32)
    grad_gate_gain = jnp.sum(grad_mixed * gated_rows * scaling_gate, axis=0)
    grad_gated = scaling_gate * gain_grad - gated_rows * scaling_gate**3 * cross_sum[:, None] / DI
    grad_gate_b = (grad_gated * mixed_rows * silu_grad(gate_pre)).astype(half)
    grad_ssd = grad_gated * gate_act
    grad_skip = jnp.sum(jnp.sum(grad_ssd * inner_x, axis=0).reshape(head_local, P_SIZE), -1)
    grad_direct = lax.dot_general(
        grad_ssd * decay_lane, c_rows, (((0,), (0,)), ((), ())), precision=highest
    )
    grad_end = prefix(
        (device_log, grad_direct), "seq", combine_states, (zero_log, zero_state), True
    )[1]
    grad_x, grad_b, grad_c, grad_cols, grad_rows_dt = ssd_backward(
        conv_all, cols, rows, grad_ssd, state_in, grad_end
    )
    grad_x, out_sum = lax.optimization_barrier((grad_x, out_sum))
    block_out = (block_f + out_sum.astype(jnp.float32)).astype(half)

    def per_head(values):
        return values.transpose(0, 2, 1).reshape(head_local, tokens)

    row_dt = grad_rows_dt.reshape(head_local, tokens)
    grad_dt_t = row_dt + per_head(grad_cols[:, :, 2:])
    steps_dt_t = rows[:, 2:].reshape(head_local, tokens)
    grad_cum_t = per_head(grad_cols[:, :, :2]) - row_dt * steps_dt_t
    grad_log_t = jnp.dot(grad_cum_t, lower, precision=highest)
    decay_rate = jnp.exp(head_params[1])[:, None]
    sigmoid_t = 1.0 - jnp.exp(-steps_dt_t)
    grad_step_t = (grad_dt_t - decay_rate * grad_log_t) * sigmoid_t
    grad_log_rate = -jnp.sum(grad_log_t * decay_rate * steps_dt_t, axis=1)
    grad_head = jnp.stack([jnp.sum(grad_step_t, axis=1), grad_log_rate, grad_skip])
    grad_act = jnp.concatenate([grad_x + skip_lane * grad_ssd, grad_b, grad_c], 1)
    grad_pre = grad_act * silu_grad(summed)
    edge_back = shifted(grad_pre[:edge_rows], "seq", -1)
    grad_ext = jnp.concatenate([grad_pre, edge_back], 0)
    grad_conv_b = sum(
        taps[k][None, :] * grad_ext[edge_rows - k : edge_rows - k + tokens] for k in range(K)
    ).astype(half)
    grad_taps = jnp.stack(
        [jnp.sum(padded[k : k + tokens] * grad_pre, axis=0) for k in range(K)]
        + [jnp.sum(grad_pre, axis=0)]
    )
    grad_inner_b = grad_conv_b[:, :inner_local]
    grad_bc_b = grad_conv_b[:, inner_local:]
    grad_step_b = grad_step_t.T.astype(half)
    both_b = jnp.concatenate([grad_gate_b, grad_inner_b], 1)
    grad_normed = (
        dot_last(both_b, zx_full)
        + jnp.dot(grad_bc_b, bc_t, preferred_element_type=jnp.float32)
        + dot_last(grad_step_b, dt_full)
    )
    bc_partial = dot_first(grad_bc_b, normed_b)
    bcconv_rows = jnp.pad(grad_taps[:, inner_local:], ((0, -(K + 1) % 8), (0, D - 2 * N)))
    summed_heads = lax.psum(
        jnp.concatenate([grad_normed, bc_partial, bcconv_rows], 0).astype(half), "head"
    ).astype(jnp.float32)
    grad_normed = summed_heads[:tokens]
    row_block = D // lax.axis_size("head")
    bc_own = lax.dynamic_slice_in_dim(
        summed_heads[tokens : tokens + 2 * N], lax.axis_index("head") * row_block, row_block, 1
    )
    grad_in_cat = jnp.concatenate(
        [
            dot_first(normed_b, both_b),
            jnp.pad(dot_first(normed_b, grad_step_b), ((0, 0), (0, spare))),
        ],
        1,
    )
    g_in_cat = lax.psum_scatter(grad_in_cat, shards, scatter_dimension=0, tiled=True)
    g_bc = lax.psum_scatter(bc_own, shards, scatter_dimension=0, tiled=True).T
    scaled_grad = grad_normed * norm_gain[None, :]
    grad_norm_gain = jnp.sum(grad_normed * block_f * scaling_in, axis=0)
    in_rows = (
        grad_f
        + scaling_in * scaled_grad
        - block_f * scaling_in**3 * jnp.sum(scaled_grad * block_f, axis=-1, keepdims=True) / D
    )
    g_zx = jnp.stack([g_in_cat[:, :inner_local], g_in_cat[:, inner_local : 2 * inner_local]])
    g_dt = g_in_cat[:, 2 * inner_local : 2 * inner_local + head_local]
    g_out = g_out_t.T
    grad_chan = jnp.concatenate([grad_taps[:, :inner_local], grad_gate_gain[None, :]], 0)
    grad_bcconv = summed_heads[tokens + 2 * N : tokens + 2 * N + K + 1, : 2 * N]
    g_gain, g_chan, g_head, g_bcconv = lax.psum(
        (grad_norm_gain, grad_chan, grad_head, grad_bcconv), shards
    )
    new_gain, nf_gain, ns_gain = adamw(
        norm_gain, g_gain, first_norm_gain, second_norm_gain, rate_vector, 0.0
    )
    new_zx, nf_zx, ns_zx = adamw(
        in_proj, g_zx, first_in_proj, second_in_proj, rate_matrix, decay_matrix
    )
    new_bc, nf_bc, ns_bc = adamw(
        bc_proj, g_bc, first_bc_proj, second_bc_proj, rate_matrix, decay_matrix
    )
    new_dt, nf_dt, ns_dt = adamw(
        dt_proj, g_dt, first_dt_proj, second_dt_proj, rate_matrix, decay_matrix
    )
    new_out, nf_out, ns_out = adamw(
        out_proj, g_out, first_out_proj, second_out_proj, rate_matrix, decay_matrix
    )
    new_chan, nf_chan, ns_chan = adamw(
        chan_params, g_chan, first_chan_params, second_chan_params, rate_vector, 0.0
    )
    new_head, nf_head, ns_head = adamw(
        head_params, g_head, first_head_params, second_head_params, rate_vector, 0.0
    )
    new_bcconv, nf_bcconv, ns_bcconv = adamw(
        bc_conv, g_bcconv, first_bc_conv, second_bc_conv, rate_vector, 0.0
    )
    return (
        block_out[None],
        in_rows[None],
        g_gain,
        g_zx,
        g_bc,
        g_dt,
        g_out,
        g_chan,
        g_head,
        g_bcconv,
        new_gain,
        new_zx,
        new_bc,
        new_dt,
        new_out,
        new_chan,
        new_head,
        new_bcconv,
        nf_gain,
        ns_gain,
        nf_zx,
        ns_zx,
        nf_bc,
        ns_bc,
        nf_dt,
        ns_dt,
        nf_out,
        ns_out,
        nf_chan,
        ns_chan,
        nf_head,
        ns_head,
        nf_bcconv,
        ns_bcconv,
    )


def solution(mesh):
    in_specs = (
        P("batch", "seq", None),
        P("batch", "seq", None),
        P(),
        P(None, ("seq", "batch"), "head"),
        P("head", ("seq", "batch")),
        P(("seq", "batch"), "head"),
        P("head", ("seq", "batch")),
        P(None, "head"),
        P(None, "head"),
        P(),
        P(),
        P(),
        P(None, ("seq", "batch"), "head"),
        P(None, ("seq", "batch"), "head"),
        P("head", ("seq", "batch")),
        P("head", ("seq", "batch")),
        P(("seq", "batch"), "head"),
        P(("seq", "batch"), "head"),
        P("head", ("seq", "batch")),
        P("head", ("seq", "batch")),
        P(None, "head"),
        P(None, "head"),
        P(None, "head"),
        P(None, "head"),
        P(),
        P(),
    )
    out_specs = (
        P("batch", "seq", None),
        P("batch", "seq", None),
        P(),
        P(None, ("seq", "batch"), "head"),
        P("head", ("seq", "batch")),
        P(("seq", "batch"), "head"),
        P("head", ("seq", "batch")),
        P(None, "head"),
        P(None, "head"),
        P(),
        P(),
        P(None, ("seq", "batch"), "head"),
        P("head", ("seq", "batch")),
        P(("seq", "batch"), "head"),
        P("head", ("seq", "batch")),
        P(None, "head"),
        P(None, "head"),
        P(),
        P(),
        P(),
        P(None, ("seq", "batch"), "head"),
        P(None, ("seq", "batch"), "head"),
        P("head", ("seq", "batch")),
        P("head", ("seq", "batch")),
        P(("seq", "batch"), "head"),
        P(("seq", "batch"), "head"),
        P("head", ("seq", "batch")),
        P("head", ("seq", "batch")),
        P(None, "head"),
        P(None, "head"),
        P(None, "head"),
        P(None, "head"),
        P(),
        P(),
    )
    return jax.shard_map(
        per_device, mesh=mesh, in_specs=in_specs, out_specs=out_specs, check_vma=False
    )
```

profile of v0, /device:TPU:1, one launch (start us, length us, event | category | flops | bytes accessed | tf_op | source)
XLA Modules:
  0.0 366.3 jit_solution(1167019068426176055)
XLA Ops:
  7.3 1.0 convert.17
  8.4 0.7 convert_element_type.77
  9.2 0.8 convert_bitcast_fusion.1
  10.0 7.1 %all-gather.2 = bf16[4,192,32]{1,2,0:T(8,128)(2,1)S(1)} all-gather(bf16[1,192,32]{1,2,0:T(8,128)(2,1)S(1)} %convert_bitcast_fusion.1), channel_id=1, replica_groups=mesh['seq'=2,'head'=4,'batch'=4] {'head'}, dimensions={0}, use_global_device_ids=true | all-gather | bytes 61440 | tf_op jit(solution)/shard_map/all_gather | solution.py:317
  17.3 0.9 bitcast_dynamic-update-slice_fusion
  18.2 0.7 copy-done.30
  20.0 0.6 multiply_multiply_fusion.8
  20.6 32.6 %all-gather.6.cloned.1.call-done = bf16[768,1536]{1,0:T(8,128)(2,1)} async-done(((bf16[96,1536]{1,0:T(8,128)(2,1)}), bf16[768,1536]{1,0:T(8,128)(2,1)}) %all-gather.6.cloned.1.call-update) | async-done | bytes 2359312 | tf_op jit(solution)/shard_map/all_gather | solution.py:329
  53.2 1.0 slice.179
  55.2 2.3 fusion.36
  57.6 1.3 collective-permute-start
  58.9 1.3 compare_select_fusion
  60.8 1.5 fusion.74
  63.0 2.6 all-gather.3
  65.7 1.8 fusion.29
  67.5 6.6 %shard_map.513 = (f32[512,384]{1,0:T(8,128)S(1)}, f32[384,128]{1,0:T(8,128)S(1)}) custom-call(f32[512,640]{1,0:T(8,128)S(1)} %get-tuple-element.390.x_ref.b_ref.c_ref, f32[512,640]{1,0:T(8,128)S(1)} %get-tuple-element.390.x_ref.b_ref.c_ref, f32[512,640]{1,0:T(8,128)S(1)} %get-tuple-element.390.x_ref.b_ref.c_ref, f32[3,512,4]{2,1,0:T(8,128)S(1)} %copy.173.cols_ref, ...), custom_call_target="tpu_custom_call" | custom-call | tf_op jit(solution)/shard_map/pallas_call | solution.py:213
  74.1 2.1 all-gather
  76.5 2.2 fusion.31
  78.7 3.2 multiply_reduce_fusion.7
  81.9 7.8 %psum.49 = f32[2,512]{1,0:T(2,128)S(1)} all-reduce(f32[2,512]{1,0:T(2,128)S(1)} %pad_maximum_fusion.8), channel_id=1, replica_groups=mesh['seq'=2,'head'=4,'batch'=4] {'head'}, use_global_device_ids=true, to_apply=%region_5.6 | all-reduce | flops 1024 | bytes 8192 | tf_op jit(solution)/shard_map/psum | solution.py:380
  89.8 3.9 %multiply_reduce_fusion.4 = (f32[384]{0:T(512)}, f32[512,384]{1,0:T(8,128)S(1)}, bf16[512,384]{1,0:T(8,128)(2,1)}, f32[384]{0:T(512)}) fusion(f32[512,640]{1,0:T(8,128)S(1)} %get-tuple-element.390.x_ref.b_ref.c_ref, f32[512,768]{1,0:T(8,128)} %copy-done.22, f32[512]{0:T(512)S(1)} %bitcast.169, f32[512,384]{1,0:T(8,128)} %get-tuple-element.389, ...), kind=kLoop, calls=%fused_computation.77 | loop fusion | flops 4521216 | bytes 5122560 | tf_op jit(solution)/shard_map/reduce_sum | solution.py:396
  93.7 1.4 fusion.44
  95.1 4.1 %all-gather.1 = f32[768,128]{1,0:T(8,128)S(1)} all-gather(f32[384,128]{1,0:T(8,128)S(1)} %fusion.44), channel_id=3, replica_groups=mesh['seq'=2,'head'=4,'batch'=4] {'seq'}, dimensions={0}, use_global_device_ids=true | all-gather | bytes 589824 | tf_op jit(solution)/shard_map/all_gather | solution.py:37
  99.2 2.7 convolution_convert_fusion
  102.0 0.7 copy-done.9
  102.7 15.8 %shard_map.514 = (f32[512,384]{1,0:T(8,128)S(1)}, f32[512,128]{1,0:T(8,128)S(1)}, f32[512,128]{1,0:T(8,128)S(1)}, f32[3,512,4]{2,1,0:T(8,128)S(1)}, f32[3,2,512]{2,1,0:T(2,128)S(1)}) custom-call(f32[512,640]{1,0:T(8,128)S(1)} %get-tuple-element.390.x_ref.b_ref.c_ref, f32[512,640]{1,0:T(8,128)S(1)} %get-tuple-element.390.x_ref.b_ref.c_ref, ...), custom_call_target="tpu_custom_call" | custom-call | tf_op jit(solution)/shard_map/pallas_call | solution.py:237
  118.5 0.9 copy-done
  119.4 0.9 copy-done.1
  120.3 2.5 slice_bitcast_fusion.1
  123.1 1.5 copy.175
  124.6 23.1 %all-reduce.7.cloned.1.call-done = bf16[512,768]{1,0:T(8,128)(2,1)} async-done(((bf16[512,768]{1,0:T(8,128)(2,1)}), bf16[512,768]{1,0:T(8,128)(2,1)}) %all-reduce.7.cloned.1.call-update) | async-done | bytes 786448 | tf_op jit(solution)/shard_map/psum | solution.py:387
  147.9 1.0 copy-done.6
  149.0 2.3 fusion.110
  151.4 1.0 copy-done.17
  152.4 2.7 collective-permute-start.1
  155.9 3.8 %fusion.25 = bf16[512,640]{1,0:T(8,128)(2,1)S(1)} fusion(f32[3,640]{1,0:T(4,128)S(1)} %collective-permute-done.1, f32[512,640]{1,0:T(8,128)} %copy-done.17, f32[640]{0:T(1024)S(1)} %get-tuple-element.333, f32[640]{0:T(1024)S(1)} %get-tuple-element.334, f32[640]{0:T(1024)S(1)} %get-tuple-element.331, f32[640]{0:T(1024)S(1)} %get-tuple-element.332), kind=kLoop, calls=%fused_computation.44 | loop fusion | flops 3604480 | bytes 1984000 | tf_op jit(solution)/shard_map/convert_element_type | solution.py:428
  161.0 1.0 copy-done.28
  162.1 0.8 fusion.34
  163.3 1.1 fusion.32
  164.8 1.7 convolution_bitcast_fusion
  166.5 1.4 copy.185
  168.4 50.4 %all-reduce.9.cloned.1.call-done = bf16[776,768]{1,0:T(8,128)(2,1)} async-done(((bf16[776,768]{1,0:T(8,128)(2,1)}), bf16[776,768]{1,0:T(8,128)(2,1)}) %all-reduce.9.cloned.1.call-update) | async-done | bytes 1191952 | tf_op jit(solution)/shard_map/psum | solution.py:444
  218.8 1.0 slice.202
  219.9 0.8 constant_dynamic-slice_fusion
  220.8 0.9 fusion.51
  221.7 1.8 select_maximum_fusion
  223.5 3.4 copy.183
  226.9 0.7 copy-done.54
  228.5 1.3 copy-done.7
  229.8 0.6 fusion.17
  230.5 30.7 %all-reduce.3 = (f32[768]{0:T(1024)S(1)}, f32[6,384]{1,0:T(8,128)S(1)}, f32[3,6]{1,0:T(4,128)S(1)}, f32[5,256]{1,0:T(8,128)S(1)}) all-reduce(f32[768]{0:T(1024)S(1)} %get-tuple-element.318, f32[6,384]{1,0:T(8,128)S(1)} %pad_maximum_fusion.7, ...), channel_id=1, replica_groups=mesh['seq'=2,'head'=4,'batch'=4] {'seq','batch'}, use_global_device_ids=true, to_apply=%region_17.18 | all-reduce | flops 4370 | bytes 34960 | tf_op jit(solution)/shard_map/psum | solution.py:473
  261.2 0.6 multiply_subtract_fusion.8
  261.9 0.6 multiply_subtract_fusion.7
  262.5 0.6 multiply_subtract_fusion.5
  263.1 0.6 multiply_subtract_fusion.4
  263.9 3.7 fusion.14
  267.6 1.8 multiply_subtract_fusion.2
  269.4 24.2 %reduce-scatter.8.cloned.1.call-done = f32[32,192]{1,0:T(8,128)} async-done(((f32[256,192]{1,0:T(8,128)}), f32[32,192]{1,0:T(8,128)}) %reduce-scatter.8.cloned.1.call-update) | async-done | bytes 24592 | tf_op jit(solution)/shard_map/reduce_scatter | solution.py:460
  293.6 1.4 multiply_subtract_fusion.3
  295.1 60.8 %reduce-scatter.10.cloned.1.call-done = f32[96,896]{1,0:T(8,128)} async-done(((f32[768,896]{1,0:T(8,128)}), f32[96,896]{1,0:T(8,128)}) %reduce-scatter.10.cloned.1.call-update) | async-done | bytes 344080 | tf_op jit(solution)/shard_map/reduce_scatter | solution.py:459
  355.8 0.8 slice.203
  356.7 0.6 multiply_subtract_fusion.6
  357.3 1.0 slice_bitcast_fusion.3
  358.4 1.1 multiply_subtract_fusion.1
  (215 shorter events, 9.3 us)
Async XLA Ops:
  7.2 11.8 %copy-start.58 = (f32[3,6]{1,0:T(4,128)S(1)}, f32[3,6]{1,0:T(4,128)}, u32[]{:S(2)}) copy-start(f32[3,6]{1,0:T(4,128)} %param.38) | copy-start | bytes 220
  7.2 12.5 %copy-start.44 = (f32[5,256]{1,0:T(8,128)S(1)}, f32[5,256]{1,0:T(8,128)}, u32[]{:S(2)}) copy-start(f32[5,256]{1,0:T(8,128)} %param.39) | copy-start | bytes 15364
  7.2 12.5 %copy-start.40 = (f32[6,384]{1,0:T(8,128)S(1)}, f32[6,384]{1,0:T(8,128)}, u32[]{:S(2)}) copy-start(f32[6,384]{1,0:T(8,128)} %param.37) | copy-start | bytes 27652
  7.2 12.5 %copy-start.13 = (bf16[1,512,768]{2,1,0:T(8,128)(2,1)S(1)}, bf16[1,512,768]{2,1,0:T(8,128)(2,1)}, u32[]{:S(2)}) copy-start(bf16[1,512,768]{2,1,0:T(8,128)(2,1)} %param.30) | copy-start | bytes 2359300
  7.3 46.0 %all-gather.6.cloned.1.call-start = ((), (), s32[]{:S(2)}) async-start(), calls=%async_computation.3 | async-start | bytes 2654208 | tf_op jit(solution)/shard_map/all_gather | solution.py:329
  17.2 37.2 %copy-start.41 = (f32[768]{0:T(1024)S(1)}, f32[768]{0:T(1024)}, u32[]{:S(2)}) copy-start(f32[768]{0:T(1024)} %param.32) | copy-start | bytes 9220
  19.0 128.8 %all-reduce.7.cloned.1.call-start = ((), (), s32[]{:S(2)}) async-start(), calls=%async_computation.4 | async-start | bytes 1572864 | tf_op jit(solution)/shard_map/psum | solution.py:387
  19.7 56.8 %copy-start.45 = (f32[384]{0:T(512)}, f32[384]{0:T(512)S(1)}, u32[]{:S(2)}) copy-start(f32[384]{0:T(512)S(1)} %mul.611) | copy-start | bytes 4612
  55.2 10.5 %copy-start.10 = (f32[512,256]{1,0:T(8,128)}, f32[512,256]{1,0:T(8,128)S(1)}, u32[]{:S(2)}) copy-start(f32[512,256]{1,0:T(8,128)S(1)} %fusion.39) | copy-start | bytes 1572868
  57.5 2.8 copy-start.22
  57.6 8.1 %copy-start.5 = (f32[512,384]{1,0:T(8,128)}, f32[512,384]{1,0:T(8,128)S(1)}, u32[]{:S(2)}) copy-start(f32[512,384]{1,0:T(8,128)S(1)} %slice.178) | copy-start | bytes 2359300
  57.6 8.0 %collective-permute-start = (f32[3,640]{1,0:T(4,128)S(1)}, f32[3,640]{1,0:T(4,128)S(1)}, u32[]{:S(2)}, u32[]{:S(2)}) collective-permute-start(f32[3,640]{1,0:T(4,128)S(1)} %fusion.83), channel_id=1, source_target_pairs={{0,16},{1,17},{2,18},{3,19},{4,20},{5,21},{6,22},{7,23},{8,24},{9,... | collective-permute-start | bytes 23048 | tf_op jit(solution)/shard_map/ppermute | solution.py:30
  60.3 2.2 copy-start.69
  76.4 5.5 %copy-start.8 = (f32[384,128]{1,0:T(8,128)}, f32[384,128]{1,0:T(8,128)S(1)}, u32[]{:S(2)}) copy-start(f32[384,128]{1,0:T(8,128)S(1)} %get-tuple-element.173.state_ref) | copy-start | bytes 589828
  76.5 2.2 copy-start.19
  76.5 2.2 copy-start.23
  78.7 3.2 copy-start.21
  89.8 3.9 %copy-start.12 = (f32[512,384]{1,0:T(8,128)S(1)}, f32[512,384]{1,0:T(8,128)}, u32[]{:S(2)}) copy-start(f32[512,384]{1,0:T(8,128)} %fusion.74) | copy-start | bytes 2359300
  93.7 5.5 %copy-start.15 = (f32[512,384]{1,0:T(8,128)S(1)}, f32[512,384]{1,0:T(8,128)}, u32[]{:S(2)}) copy-start(f32[512,384]{1,0:T(8,128)} %get-tuple-element.389) | copy-start | bytes 2359300
  101.9 116.9 %all-reduce.9.cloned.1.call-start = ((), (), s32[]{:S(2)}) async-start(), calls=%async_computation.5 | async-start | bytes 2383872 | tf_op jit(solution)/shard_map/psum | solution.py:444
  122.8 24.9 %copy-start.2 = (f32[512,384]{1,0:T(8,128)S(1)}, f32[512,384]{1,0:T(8,128)}, u32[]{:S(2)}) copy-start(f32[512,384]{1,0:T(8,128)} %copy-done.1) | copy-start | bytes 2359300
  122.8 25.0 %copy-start.46 = (f32[384]{0:T(512)S(1)}, f32[384]{0:T(512)}, u32[]{:S(2)}) copy-start(f32[384]{0:T(512)} %copy-done.45) | copy-start | bytes 4612
  123.1 24.8 %copy-start.4 = (f32[515,640]{1,0:T(8,128)S(1)}, f32[515,640]{1,0:T(8,128)}, u32[]{:S(2)}) copy-start(f32[515,640]{1,0:T(8,128)} %copy-done.3) | copy-start | bytes 3955204
  149.0 6.1 %copy-start.68 = (f32[6]{0:T(128)S(1)}, f32[6]{0:T(128)}, u32[]{:S(2)}) copy-start(f32[6]{0:T(128)} %get-tuple-element.407) | copy-start | bytes 76
  149.0 6.1 %copy-start.70 = (f32[512,6]{0,1:T(8,128)S(1)}, f32[512,6]{0,1:T(8,128)}, u32[]{:S(2)}) copy-start(f32[512,6]{0,1:T(8,128)} %copy-done.69) | copy-start | bytes 36868
  151.3 8.3 %copy-start.14 = (bf16[1,512,768]{2,1,0:T(8,128)(2,1)S(1)}, bf16[1,512,768]{2,1,0:T(8,128)(2,1)}, u32[]{:S(2)}) copy-start(bf16[1,512,768]{2,1,0:T(8,128)(2,1)} %param.30) | copy-start | bytes 2359300
  152.4 3.5 collective-permute-start.1
  160.2 1.8 copy-start.28
  160.2 1.9 copy-start.31
  160.7 2.2 copy-start.33
  164.4 103.1 %reduce-scatter.12.cloned.1.call-start = ((), (), s32[]{:S(2)}) async-start(), calls=%async_computation.8 | async-start | bytes 1327104 | tf_op jit(solution)/shard_map/reduce_scatter | solution.py:388
  168.0 125.7 %reduce-scatter.8.cloned.1.call-start = ((), (), s32[]{:S(2)}) async-start(), calls=%async_computation.6 | async-start | bytes 294912 | tf_op jit(solution)/shard_map/reduce_scatter | solution.py:460
  168.0 52.8 %copy-start.32 = (bf16[512,384]{1,0:T(8,128)(2,1)S(1)}, bf16[512,384]{1,0:T(8,128)(2,1)}, u32[]{:S(2)}) copy-start(bf16[512,384]{1,0:T(8,128)(2,1)} %get-tuple-element.392) | copy-start | bytes 1179652
  168.0 52.8 %copy-start.34 = (bf16[512,384]{1,0:T(8,128)(2,1)S(1)}, bf16[512,384]{1,0:T(8,128)(2,1)}, u32[]{:S(2)}) copy-start(bf16[512,384]{1,0:T(8,128)(2,1)} %copy-done.33) | copy-start | bytes 1179652
  220.7 135.1 %reduce-scatter.10.cloned.1.call-start = ((), (), s32[]{:S(2)}) async-start(), calls=%async_computation.7 | async-start | bytes 3096576 | tf_op jit(solution)/shard_map/reduce_scatter | solution.py:459
  228.3 32.9 %copy-start.59 = (f32[3,6]{1,0:T(4,128)S(1)}, f32[3,6]{1,0:T(4,128)}, u32[]{:S(2)}) copy-start(f32[3,6]{1,0:T(4,128)} %param.38) | copy-start | bytes 220
  228.4 32.9 %copy-start.65 = (f32[3,6]{1,0:T(4,128)S(1)}, f32[3,6]{1,0:T(4,128)}, u32[]{:S(2)}) copy-start(f32[3,6]{1,0:T(4,128)} %param.52) | copy-start | bytes 220
  228.4 32.9 %copy-start.66 = (f32[3,6]{1,0:T(4,128)S(1)}, f32[3,6]{1,0:T(4,128)}, u32[]{:S(2)}) copy-start(f32[3,6]{1,0:T(4,128)} %param.53) | copy-start | bytes 220
  228.4 33.5 %copy-start.60 = (f32[768]{0:T(1024)S(1)}, f32[768]{0:T(1024)}, u32[]{:S(2)}) copy-start(f32[768]{0:T(1024)} %param.40) | copy-start | bytes 9220
  228.4 33.5 %copy-start.61 = (f32[768]{0:T(1024)S(1)}, f32[768]{0:T(1024)}, u32[]{:S(2)}) copy-start(f32[768]{0:T(1024)} %param.41) | copy-start | bytes 9220
  228.4 34.1 %copy-start.55 = (f32[5,256]{1,0:T(8,128)S(1)}, f32[5,256]{1,0:T(8,128)}, u32[]{:S(2)}) copy-start(f32[5,256]{1,0:T(8,128)} %param.54) | copy-start | bytes 15364
  228.4 34.1 %copy-start.56 = (f32[5,256]{1,0:T(8,128)S(1)}, f32[5,256]{1,0:T(8,128)}, u32[]{:S(2)}) copy-start(f32[5,256]{1,0:T(8,128)} %param.55) | copy-start | bytes 15364
  228.4 34.7 %copy-start.49 = (f32[6,384]{1,0:T(8,128)S(1)}, f32[6,384]{1,0:T(8,128)}, u32[]{:S(2)}) copy-start(f32[6,384]{1,0:T(8,128)} %param.50) | copy-start | bytes 27652
  228.4 34.7 %copy-start.50 = (f32[6,384]{1,0:T(8,128)S(1)}, f32[6,384]{1,0:T(8,128)}, u32[]{:S(2)}) copy-start(f32[6,384]{1,0:T(8,128)} %param.51) | copy-start | bytes 27652
  228.4 35.3 %copy-start.20 = (bf16[1,512,768]{2,1,0:T(8,128)(2,1)S(1)}, bf16[1,512,768]{2,1,0:T(8,128)(2,1)}, u32[]{:S(2)}) copy-start(bf16[1,512,768]{2,1,0:T(8,128)(2,1)} %param.31) | copy-start | bytes 2359300
  228.5 35.3 %copy-start.52 = (f32[512]{0:T(512)S(1)}, f32[512]{0:T(512)}, u32[]{:S(2)}) copy-start(f32[512]{0:T(512)} %get-tuple-element.405) | copy-start | bytes 6148
  229.8 33.9 %copy-start.27 = (bf16[512,768]{1,0:T(8,128)(2,1)S(1)}, bf16[512,768]{1,0:T(8,128)(2,1)}, u32[]{:S(2)}) copy-start(bf16[512,768]{1,0:T(8,128)(2,1)} %all-reduce.7.cloned.1.call-done) | copy-start | bytes 2359300
  261.2 6.3 %copy-start.51 = (f32[6,384]{1,0:T(8,128)}, f32[6,384]{1,0:T(8,128)S(1)}, u32[]{:S(2)}) copy-start(f32[6,384]{1,0:T(8,128)S(1)} %get-tuple-element.356) | copy-start | bytes 27652
  261.2 6.3 %copy-start.57 = (f32[5,256]{1,0:T(8,128)}, f32[5,256]{1,0:T(8,128)S(1)}, u32[]{:S(2)}) copy-start(f32[5,256]{1,0:T(8,128)S(1)} %get-tuple-element.358) | copy-start | bytes 15364
  261.2 6.3 %copy-start.64 = (f32[768]{0:T(1024)}, f32[768]{0:T(1024)S(1)}, u32[]{:S(2)}) copy-start(f32[768]{0:T(1024)S(1)} %get-tuple-element.355) | copy-start | bytes 9220
  261.2 6.3 %copy-start.67 = (f32[3,6]{1,0:T(4,128)}, f32[3,6]{1,0:T(4,128)S(1)}, u32[]{:S(2)}) copy-start(f32[3,6]{1,0:T(4,128)S(1)} %get-tuple-element.357) | copy-start | bytes 220
  263.7 3.9 %copy-start.29 = (f32[384,96]{0,1:T(8,128)S(1)}, f32[384,96]{0,1:T(8,128)}, u32[]{:S(2)}) copy-start(f32[384,96]{0,1:T(8,128)} %param.36) | copy-start | bytes 442372
  263.8 3.9 %copy-start.37 = (f32[384,96]{0,1:T(8,128)S(1)}, f32[384,96]{0,1:T(8,128)}, u32[]{:S(2)}) copy-start(f32[384,96]{0,1:T(8,128)} %param.48) | copy-start | bytes 442372
  263.8 3.9 %copy-start.38 = (f32[384,96]{0,1:T(8,128)S(1)}, f32[384,96]{0,1:T(8,128)}, u32[]{:S(2)}) copy-start(f32[384,96]{0,1:T(8,128)} %param.49) | copy-start | bytes 442372
  263.8 29.9 %copy-start.39 = (f32[192,32]{0,1:T(8,128)S(1)}, f32[192,32]{0,1:T(8,128)}, u32[]{:S(2)}) copy-start(f32[192,32]{0,1:T(8,128)} %param.34) | copy-start | bytes 73732
  263.8 29.9 %copy-start.42 = (f32[192,32]{0,1:T(8,128)S(1)}, f32[192,32]{0,1:T(8,128)}, u32[]{:S(2)}) copy-start(f32[192,32]{0,1:T(8,128)} %param.44) | copy-start | bytes 73732
  263.8 29.8 %copy-start.43 = (f32[192,32]{0,1:T(8,128)S(1)}, f32[192,32]{0,1:T(8,128)}, u32[]{:S(2)}) copy-start(f32[192,32]{0,1:T(8,128)} %param.45) | copy-start | bytes 73732
  263.8 92.9 %copy-start.47 = (f32[96,6]{0,1:T(8,128)S(1)}, f32[96,6]{0,1:T(8,128)}, u32[]{:S(2)}) copy-start(f32[96,6]{0,1:T(8,128)} %param.35) | copy-start | bytes 6916
  263.8 92.9 %copy-start.62 = (f32[96,6]{0,1:T(8,128)S(1)}, f32[96,6]{0,1:T(8,128)}, u32[]{:S(2)}) copy-start(f32[96,6]{0,1:T(8,128)} %param.46) | copy-start | bytes 6916
  263.8 92.8 %copy-start.63 = (f32[96,6]{0,1:T(8,128)S(1)}, f32[96,6]{0,1:T(8,128)}, u32[]{:S(2)}) copy-start(f32[96,6]{0,1:T(8,128)} %param.47) | copy-start | bytes 6916
  267.5 90.8 %copy-start.26 = (f32[2,96,384]{2,1,0:T(8,128)S(1)}, f32[2,96,384]{2,1,0:T(8,128)}, u32[]{:S(2)}) copy-start(f32[2,96,384]{2,1,0:T(8,128)} %param.33) | copy-start | bytes 884740
  267.5 90.8 %copy-start.35 = (f32[2,96,384]{2,1,0:T(8,128)S(1)}, f32[2,96,384]{2,1,0:T(8,128)}, u32[]{:S(2)}) copy-start(f32[2,96,384]{2,1,0:T(8,128)} %param.42) | copy-start | bytes 884740
  267.6 90.8 %copy-start.36 = (f32[2,96,384]{2,1,0:T(8,128)S(1)}, f32[2,96,384]{2,1,0:T(8,128)}, u32[]{:S(2)}) copy-start(f32[2,96,384]{2,1,0:T(8,128)} %param.43) | copy-start | bytes 884740
  356.7 2.7 copy-start.48
  (15 other events, 15.9 us)
Sparse Core Ops, SparseCore 0:
  19.1 34.0 all-gather.5
  102.0 45.6 all-reduce.6
  164.6 54.2 all-reduce.8
  221.5 37.8 reduce-scatter.11
  262.0 31.5 reduce-scatter.7
  295.8 59.9 reduce-scatter.9
where the time goes:
time: 367 us; the launch traced here: 366 us
  waiting for transfers between devices  192 us (52%)
  blocking collectives  54.4 us (15%)
  other arithmetic  31.9 us (9%)
  local copies, waits for them, and re-layouts  25.4 us (7%)
  Pallas kernels  22.4 us (6%)
  matrix products  21 us (6%)
  between operations  15.2 us (4%)
  starting transfers between devices  4.44 us (1%)
    reduce_scatter x1, waiting for transfers between devices, per_device(): lax.psum_scatter(grad_in_cat, shards, scatter_dimension=0, tiled=True)  60.8 us
    psum x1, waiting for transfers between devices, per_device(): lax.psum(jnp.concatenate([grad_normed, bc_partial, bcconv_rows], 0).astyp...  50.4 us
    all_gather x1, waiting for transfers between devices, per_device(): full = lax.all_gather(packed, shards, axis=0, tiled=True)  32.6 us
    psum x1, blocking collectives, per_device(): lax.psum((grad_norm_gain, grad_chan, grad_head, grad_bcconv), shards)  30.7 us
    reduce_scatter x1, waiting for transfers between devices, per_device(): g_bc = lax.psum_scatter(bc_own, shards, scatter_dimension=0, tiled=True).T  24.2 us
    psum x1, waiting for transfers between devices, per_device(): out_sum = lax.psum(out_partial.astype(half), 'head')  23.1 us
    pallas_call x1, Pallas kernels, ssd_backward(): pl.pallas_call(backward_kernel, grid=(pairs,), in_specs=common_specs(toke...  15.8 us
    unnamed x152, local copies, waits for them, and re-layouts  15 us
  transfers between devices with their start and end apart: 8, of which 6 were waited for; matrix products, arithmetic and copies ran while one was open for 9% of the time, Pallas kernels for 4%

commit v1 on v0

--- a/solution.py
+++ b/solution.py
@@ -1,3 +1,5 @@
+import functools
+
 import jax
 import jax.numpy as jnp
 from jax import lax
@@ -259,6 +261,153 @@
         ],
         compiler_params=pltpu.CompilerParams(vmem_limit_bytes=32 << 20),
     )(conv_all, conv_all, conv_all, cols, rows, grad_ssd, state_in, grad_end)
+
+
+def greet(peers):
+    barrier = pltpu.get_barrier_semaphore()
+    for peer in peers:
+        pl.semaphore_signal(
+            barrier, inc=1, device_id=peer, device_id_type=pl.DeviceIdType.MESH
+        )
+    pl.semaphore_wait(barrier, len(peers))
+
+
+def head_sum_kernel(count, x_ref, out_ref, slots, total, send_one, recv_one, send_two, recv_two):
+    me = lax.axis_index("head")
+    rows = x_ref.shape[0] // count
+    peers = [lax.rem(me + lap, count) for lap in range(1, count)]
+    greet([{"head": peer} for peer in peers])
+
+    def span(place):
+        return pl.ds(pl.multiple_of(place * rows, 16), rows)
+
+    first = [
+        pltpu.make_async_remote_copy(
+            src_ref=x_ref.at[span(peer)],
+            dst_ref=slots.at[lap],
+            send_sem=send_one.at[lap],
+            recv_sem=recv_one.at[lap],
+            device_id={"head": peer},
+            device_id_type=pl.DeviceIdType.MESH,
+        )
+        for lap, peer in enumerate(peers)
+    ]
+    for copy in first:
+        copy.start()
+    acc = x_ref[span(me), :].astype(jnp.float32)
+    for lap, copy in enumerate(first):
+        copy.wait()
+        acc = acc + slots[lap].astype(jnp.float32)
+    total[...] = acc.astype(total.dtype)
+    out_ref[span(me), :] = total[...]
+    second = [
+        pltpu.make_async_remote_copy(
+            src_ref=total,
+            dst_ref=out_ref.at[span(me)],
+            send_sem=send_two.at[lap],
+            recv_sem=recv_two.at[lap],
+            device_id={"head": peer},
+            device_id_type=pl.DeviceIdType.MESH,
+        )
+        for lap, peer in enumerate(peers)
+    ]
+    for copy in second:
+        copy.start()
+    for copy in second:
+        copy.wait()
+
+
+def head_sum(values):
+    count = lax.axis_size("head")
+    if count == 1:
+        return values
+    rows, width = values.shape
+    vmem = pl.BlockSpec(memory_space=pltpu.VMEM)
+    sems = pltpu.SemaphoreType.DMA((count - 1,))
+    return pl.pallas_call(
+        functools.partial(head_sum_kernel, count),
+        out_shape=jax.ShapeDtypeStruct(values.shape, values.dtype),
+        in_specs=[vmem],
+        out_specs=vmem,
+        scratch_shapes=[
+            pltpu.VMEM((count - 1, rows // count, width), values.dtype),
+            pltpu.VMEM((rows // count, width), values.dtype),
+            sems,
+            sems,
+            sems,
+            sems,
+        ],
+        compiler_params=pltpu.CompilerParams(
+            collective_id=0, has_side_effects=True, vmem_limit_bytes=16 << 20
+        ),
+    )(values)
+
+
+def shard_sum_kernel(
+    counts, small_ref, part_ref, small_out, part_out,
+    small_slots, part_slots, send_one, recv_one, send_two, recv_two,
+):
+    seqs, batches = counts
+    count = seqs * batches
+    me = lax.axis_index("seq") * batches + lax.axis_index("batch")
+    places = [lax.rem(me + lap, count) for lap in range(1, count)]
+    peers = [
+        {"seq": lax.div(place, batches), "batch": lax.rem(place, batches)} for place in places
+    ]
+    greet(peers)
+    copies = []
+    for lap, (place, peer) in enumerate(zip(places, peers)):
+        for source, slots, send, recv in (
+            (small_ref, small_slots, send_one, recv_one),
+            (part_ref.at[place], part_slots, send_two, recv_two),
+        ):
+            copies.append(
+                pltpu.make_async_remote_copy(
+                    src_ref=source,
+                    dst_ref=slots.at[me],
+                    send_sem=send.at[lap],
+                    recv_sem=recv.at[lap],
+                    device_id=peer,
+                    device_id_type=pl.DeviceIdType.MESH,
+                )
+            )
+    for copy in copies:
+        copy.start()
+    small_slots[me] = small_ref[...]
+    part_slots[me] = part_ref[me]
+    for copy in copies:
+        copy.wait()
+    small_out[...] = sum(small_slots[place] for place in range(count))
+    part_out[...] = sum(part_slots[place] for place in range(count))
+
+
+def shard_sum(small, part):
+    counts = (lax.axis_size("seq"), lax.axis_size("batch"))
+    count = part.shape[0]
+    if count == 1:
+        return small, part[0]
+    vmem = pl.BlockSpec(memory_space=pltpu.VMEM)
+    sems = pltpu.SemaphoreType.DMA((count - 1,))
+    return pl.pallas_call(
+        functools.partial(shard_sum_kernel, counts),
+        out_shape=[
+            jax.ShapeDtypeStruct(small.shape, small.dtype),
+            jax.ShapeDtypeStruct(part.shape[1:], part.dtype),
+        ],
+        in_specs=[vmem, vmem],
+        out_specs=[vmem, vmem],
+        scratch_shapes=[
+            pltpu.VMEM((count,) + small.shape, small.dtype),
+            pltpu.VMEM(part.shape, part.dtype),
+            sems,
+            sems,
+            sems,
+            sems,
+        ],
+        compiler_params=pltpu.CompilerParams(
+            collective_id=1, has_side_effects=True, vmem_limit_bytes=16 << 20
+        ),
+    )(small, part)
 
 
 def combine_states(earlier, later):
@@ -386,8 +535,8 @@
     out_partial = dot_last(mixed_b, out_t)
     out_sum = lax.psum(out_partial.astype(half), "head")
     g_out_t = lax.psum_scatter(
-        dot_first(grad_rows, mixed_b), shards, scatter_dimension=0, tiled=True
-    )
+        dot_first(grad_rows, mixed_b).astype(half), shards, scatter_dimension=0, tiled=True
+    ).astype(jnp.float32)
     grad_f = grad_rows.astype(jnp.float32)
     grad_gate_gain = jnp.sum(grad_mixed * gated_rows * scaling_gate, axis=0)
     grad_gated = scaling_gate * gain_grad - gated_rows * scaling_gate**3 * cross_sum[:, None] / DI
@@ -403,7 +552,6 @@
     grad_x, grad_b, grad_c, grad_cols, grad_rows_dt = ssd_backward(
         conv_all, cols, rows, grad_ssd, state_in, grad_end
     )
-    grad_x, out_sum = lax.optimization_barrier((grad_x, out_sum))
     block_out = (block_f + out_sum.astype(jnp.float32)).astype(half)
 
     def per_head(values):
@@ -441,9 +589,9 @@
     )
     bc_partial = dot_first(grad_bc_b, normed_b)
     bcconv_rows = jnp.pad(grad_taps[:, inner_local:], ((0, -(K + 1) % 8), (0, D - 2 * N)))
-    summed_heads = lax.psum(
-        jnp.concatenate([grad_normed, bc_partial, bcconv_rows], 0).astype(half), "head"
-    ).astype(jnp.float32)
+    stacked = jnp.concatenate([grad_normed, bc_partial, bcconv_rows], 0).astype(half)
+    stacked = jnp.pad(stacked, ((0, -stacked.shape[0] % (16 * lax.axis_size("head"))), (0, 0)))
+    summed_heads = head_sum(stacked).astype(jnp.float32)
     grad_normed = summed_heads[:tokens]
     row_block = D // lax.axis_size("head")
     bc_own = lax.dynamic_slice_in_dim(
@@ -456,8 +604,9 @@
         ],
         1,
     )
-    g_in_cat = lax.psum_scatter(grad_in_cat, shards, scatter_dimension=0, tiled=True)
-    g_bc = lax.psum_scatter(bc_own, shards, scatter_dimension=0, tiled=True).T
+    g_in_cat = lax.psum_scatter(
+        grad_in_cat.astype(half), shards, scatter_dimension=0, tiled=True
+    ).astype(jnp.float32)
     scaled_grad = grad_normed * norm_gain[None, :]
     grad_norm_gain = jnp.sum(grad_normed * block_f * scaling_in, axis=0)
     in_rows = (
@@ -470,9 +619,18 @@
     g_out = g_out_t.T
     grad_chan = jnp.concatenate([grad_taps[:, :inner_local], grad_gate_gain[None, :]], 0)
     grad_bcconv = summed_heads[tokens + 2 * N : tokens + 2 * N + K + 1, : 2 * N]
-    g_gain, g_chan, g_head, g_bcconv = lax.psum(
-        (grad_norm_gain, grad_chan, grad_head, grad_bcconv), shards
-    )
+    pieces = (grad_norm_gain, grad_chan, grad_head, grad_bcconv)
+    flat = jnp.concatenate([piece.reshape(-1) for piece in pieces])
+    flat = jnp.pad(flat, (0, -flat.shape[0] % (8 * 128))).reshape(-1, 128)
+    small_sum, g_bc_t = shard_sum(flat, bc_own.reshape(D // shard_rows, -1, row_block))
+    g_bc = g_bc_t.T
+    small_sum = small_sum.reshape(-1)
+    taken = []
+    offset = 0
+    for piece in pieces:
+        taken.append(small_sum[offset : offset + piece.size].reshape(piece.shape))
+        offset += piece.size
+    g_gain, g_chan, g_head, g_bcconv = taken
     new_gain, nf_gain, ns_gain = adamw(
         norm_gain, g_gain, first_norm_gain, second_norm_gain, rate_vector, 0.0
     )

time: 367 us -> 270 us (0.74)
  waiting for transfers between devices: 192 us -> 83.1 us
  Pallas kernels: 22.4 us -> 70.3 us
  blocking collectives: 54.4 us -> 23.6 us
  local copies, waits for them, and re-layouts: 25.4 us -> 20.6 us
  other arithmetic: 31.9 us -> 27.3 us
    psum x1 -> x0, waiting for transfers between devices: 50.4 us -> none  [per_device(): lax.psum(jnp.concatenate([grad_normed, bc_partial, bcconv_rows], 0).astyp...]
    pallas_call x0 -> x2, Pallas kernels: none -> 48.7 us  [the longest x1 36.8 us: head_sum(): pl.pallas_call(functools.partial(head_sum_kernel, count), out_shape=jax.S...]
    reduce_scatter x3 -> x2, waiting for transfers between devices: 85 us -> 53.1 us  [the longest x1 36.3 us: per_device(): lax.psum_scatter(grad_in_cat.astype(half), shards, scatter_dimension=0, t...]
    psum x1 -> x0, blocking collectives: 30.7 us -> none  [per_device(): lax.psum((grad_norm_gain, grad_chan, grad_head, grad_bcconv), shards)]
    psum x1, waiting for transfers between devices: 23.1 us -> 0.01 us  [per_device(): out_sum = lax.psum(out_partial.astype(half), 'head')]
    unnamed x152 -> x121, local copies, waits for them, and re-layouts: 15 us -> 11.8 us
  transfers between devices with their start and end apart: 8 -> 6, of which waited for: 6 -> 3; matrix products, arithmetic and copies ran while one was open for 9% -> 14% of each run, Pallas kernels for 4% -> 18%
where the time goes in v1:
time: 270 us; the launch traced here: 269 us
  waiting for transfers between devices  83.1 us (31%)
  Pallas kernels  70.3 us (26%)
  other arithmetic  27.3 us (10%)
  matrix products  24.1 us (9%)
  blocking collectives  23.6 us (9%)
  local copies, waits for them, and re-layouts  20.6 us (8%)
  between operations  14.8 us (5%)
  starting transfers between devices  5.19 us (2%)
    pallas_call x1, Pallas kernels, head_sum(): pl.pallas_call(functools.partial(head_sum_kernel, count), out_shape=jax.S...  36.8 us
    reduce_scatter x1, waiting for transfers between devices, per_device(): lax.psum_scatter(grad_in_cat.astype(half), shards, scatter_dimension=0, t...  36.3 us
    all_gather x1, waiting for transfers between devices, per_device(): full = lax.all_gather(packed, shards, axis=0, tiled=True)  29.9 us
    reduce_scatter x1, waiting for transfers between devices, per_device(): lax.psum_scatter(dot_first(grad_rows, mixed_b).astype(half), shards, scat...  16.8 us
    pallas_call x1, Pallas kernels, ssd_backward(): pl.pallas_call(backward_kernel, grid=(pairs,), in_specs=common_specs(toke...  15 us
    pallas_call x1, Pallas kernels, shard_sum(): pl.pallas_call(functools.partial(shard_sum_kernel, counts), out_shape=[ja...  11.9 us
    unnamed x121, local copies, waits for them, and re-layouts  11.8 us
    sub x8, other arithmetic, adamw(): weight - step_rate * (first_hat / (jnp.sqrt(second_hat) + adam_eps) + dec...  9.65 us
  transfers between devices with their start and end apart: 6, of which 3 were waited for; matrix products, arithmetic and copies ran while one was open for 14% of the time, Pallas kernels for 18%

profile of v1, /device:TPU:1, one launch (start us, length us, event | category | flops | bytes accessed | tf_op | source)
XLA Modules:
  0.0 269.0 jit_solution(1055084583210528548)
XLA Ops:
  7.3 1.1 convert.26
  8.4 0.7 convert_element_type.92
  9.3 0.8 convert_bitcast_fusion.2
  10.0 7.1 %all-gather.2 = bf16[4,192,32]{1,2,0:T(8,128)(2,1)S(1)} all-gather(bf16[1,192,32]{1,2,0:T(8,128)(2,1)S(1)} %convert_bitcast_fusion.2), channel_id=1, replica_groups=mesh['seq'=2,'head'=4,'batch'=4] {'head'}, dimensions={0}, use_global_device_ids=true | all-gather | bytes 61440 | tf_op jit(solution)/shard_map/all_gather | solution.py:466
  17.3 0.9 bitcast_dynamic-update-slice_fusion
  18.3 0.7 copy-done.27
  19.1 0.7 copy.186
  19.8 0.5 fusion.101
  20.4 0.7 mul.611
  21.0 0.7 copy.181
  21.8 0.7 copy.179
  22.8 0.6 multiply_multiply_fusion.8
  23.4 29.9 %all-gather.6.cloned.1.call-done = bf16[768,1536]{1,0:T(8,128)(2,1)} async-done(((bf16[96,1536]{1,0:T(8,128)(2,1)}), bf16[768,1536]{1,0:T(8,128)(2,1)}) %all-gather.6.cloned.1.call-update) | async-done | bytes 2359312 | tf_op jit(solution)/shard_map/all_gather | solution.py:478
  53.3 1.0 slice.200
  55.0 2.3 fusion.39
  57.4 1.0 copy-done.20
  58.4 1.3 collective-permute-start
  59.7 1.3 compare_select_fusion
  61.6 1.5 fusion.77
  63.8 2.6 all-gather.3
  66.5 1.8 fusion.31
  68.3 6.6 %shard_map.513 = (f32[512,384]{1,0:T(8,128)S(1)}, f32[384,128]{1,0:T(8,128)S(1)}) custom-call(f32[512,640]{1,0:T(8,128)S(1)} %get-tuple-element.423.x_ref.b_ref.c_ref, f32[512,640]{1,0:T(8,128)S(1)} %get-tuple-element.423.x_ref.b_ref.c_ref, f32[512,640]{1,0:T(8,128)S(1)} %get-tuple-element.423.x_ref.b_ref.c_ref, f32[3,512,4]{2,1,0:T(8,128)S(1)} %copy.168.cols_ref, ...), custom_call_target="tpu_custom_call" | custom-call | tf_op jit(solution)/shard_map/pallas_call | solution.py:215
  75.0 2.1 all-gather
  77.3 2.2 fusion.33
  79.5 2.8 %multiply_reduce_fusion.7 = (f32[512]{0:T(512)S(1)}, f32[512]{0:T(512)S(1)}, f32[512,384]{1,0:T(8,128)S(1)}, f32[512,384]{1,0:T(8,128)}) fusion(f32[384]{0:T(512)S(1)} %slice_reduce_fusion.1, f32[512,384]{1,0:T(8,128)S(1)} %fusion.33, f32[512,768]{1,0:T(8,128)S(1)} %copy-done.21, bf16[768,1536]{1,0:T(8,128)(2,1)} %all-gather.6.cloned.1.call-done, ...), kind=kOutput, calls=%fused_computation.92 | convolution fusion | flops 303954944 | bytes 4527616 | tf_op jit(solution)/shard_map/dot_general | solution.py:527
  82.4 7.8 %psum.14 = f32[2,512]{1,0:T(2,128)S(1)} all-reduce(f32[2,512]{1,0:T(2,128)S(1)} %pad_maximum_fusion.8), channel_id=1, replica_groups=mesh['seq'=2,'head'=4,'batch'=4] {'head'}, use_global_device_ids=true, to_apply=%region_5.6 | all-reduce | flops 1024 | bytes 8192 | tf_op jit(solution)/shard_map/psum | solution.py:529
  90.3 2.7 %fusion.34 = bf16[768,384]{0,1:T(8,128)(2,1)} fusion(bf16[1,512,768]{2,1,0:T(8,128)(2,1)} %param.31, f32[512,384]{1,0:T(8,128)S(1)} %get-tuple-element.422, f32[512]{0:T(512)S(1)} %bitcast.176, f32[384]{0:T(512)S(1)} %slice_reduce_fusion.1), kind=kOutput, calls=%fused_computation.63 | convolution fusion | flops 302874624 | bytes 2166272 | tf_op jit(solution)/shard_map/dot_general | solution.py:57
  93.0 2.9 %multiply_reduce_fusion.4 = (f32[384]{0:T(512)S(1)}, f32[512,384]{1,0:T(8,128)S(1)}, bf16[512,384]{1,0:T(8,128)(2,1)}, f32[384]{0:T(512)S(1)}) fusion(f32[512,640]{1,0:T(8,128)S(1)} %get-tuple-element.423.x_ref.b_ref.c_ref, f32[512,768]{1,0:T(8,128)} %copy-done.20, f32[512]{0:T(512)S(1)} %bitcast.179, f32[512,384]{1,0:T(8,128)} %copy-done.8, ...), kind=kLoop, calls=%fused_computation.81 | loop fusion | flops 4521216 | bytes 5122560 | tf_op jit(solution)/shard_map/reduce_sum | solution.py:545
  95.9 1.4 fusion.47
  97.3 4.0 %all-gather.1 = f32[768,128]{1,0:T(8,128)} all-gather(f32[384,128]{1,0:T(8,128)S(1)} %fusion.47), channel_id=3, replica_groups=mesh['seq'=2,'head'=4,'batch'=4] {'seq'}, dimensions={0}, use_global_device_ids=true | all-gather | bytes 589824 | tf_op jit(solution)/shard_map/all_gather | solution.py:39
  101.4 15.0 %shard_map.514 = (f32[512,384]{1,0:T(8,128)S(1)}, f32[512,128]{1,0:T(8,128)S(1)}, f32[512,128]{1,0:T(8,128)S(1)}, f32[3,512,4]{2,1,0:T(8,128)S(1)}, f32[3,2,512]{2,1,0:T(2,128)S(1)}) custom-call(f32[512,640]{1,0:T(8,128)S(1)} %get-tuple-element.423.x_ref.b_ref.c_ref, f32[512,640]{1,0:T(8,128)S(1)} %get-tuple-element.423.x_ref.b_ref.c_ref, ...), custom_call_target="tpu_custom_call" | custom-call | tf_op jit(solution)/shard_map/pallas_call | solution.py:239
  116.6 1.4 copy-done.3
  118.3 1.0 fusion.111
  119.3 3.5 %collective-permute-start.1 = (f32[3,640]{1,0:T(4,128)S(1)}, f32[3,640]{1,0:T(4,128)S(1)}, u32[]{:S(2)}, u32[]{:S(2)}) collective-permute-start(f32[3,640]{1,0:T(4,128)S(1)} %slice.212), channel_id=1, source_target_pairs={{16,0},{17,1},{18,2},{19,3},{20,4},{21,5},{22,6},{23,7},{24,8},{25... | collective-permute-start | bytes 23048 | tf_op jit(solution)/shard_map/ppermute | solution.py:32
  122.9 2.6 convolution_convert_fusion.1
  127.1 1.1 copy.198
  129.5 0.6 fusion.27
  130.1 0.7 copy-done.29
  130.9 0.9 convolution_convert_fusion
  131.9 1.6 copy.196
  133.9 2.3 fusion.37
  136.7 1.4 add_convert_fusion
  138.3 36.8 %shard_map.515 = bf16[832,768]{1,0:T(8,128)(2,1)S(1)} custom-call(bf16[832,768]{1,0:T(8,128)(2,1)S(1)} %pad.24.x_ref), custom_call_target="tpu_custom_call" | custom-call | tf_op jit(solution)/shard_map/pallas_call | solution.py:327
  175.4 0.9 slice.223
  176.3 1.2 fusion.18
  177.6 1.1 constant_dynamic-slice_fusion
  178.7 11.9 %shard_map.516 = (f32[40,128]{1,0:T(8,128)S(1)}, f32[32,192]{1,0:T(8,128)S(1)}) custom-call(f32[40,128]{1,0:T(8,128)S(1)} %pad_bitcast_fusion.small_ref, f32[8,32,192]{2,1,0:T(8,128)S(1)} %bitcast.165), custom_call_target="tpu_custom_call" | custom-call | tf_op jit(solution)/shard_map/pallas_call | solution.py:391
  190.8 1.3 multiply_subtract_fusion.7
  192.2 1.3 multiply_subtract_fusion.6
  193.5 1.3 multiply_subtract_fusion.5
  194.8 1.3 multiply_subtract_fusion.4
  196.1 1.4 multiply_subtract_fusion.3
  197.6 3.5 %fusion.15 = (f32[1,512,768]{2,1,0:T(8,128)}, bf16[1,512,768]{2,1,0:T(8,128)(2,1)}) fusion(bf16[1,512,768]{2,1,0:T(8,128)(2,1)S(1)} %copy-done.12, f32[832,768]{1,0:T(8,128)S(1)} %convert_element_type.105, bf16[1,512,768]{2,1,0:T(8,128)(2,1)} %param.31, f32[512]{0:T(512)} %get-tuple-element.353, f32[512]{0:T(512)} %get-tuple-element.440, ...), kind=kLoop, calls=%fused_computation.27 | loop fusion | flops 4718592 | bytes 6300672 | tf_op jit(solution)/shard_map/broadcast_in_dim | solution.py:660
  201.1 16.8 %reduce-scatter.9.cloned.1.call-done = bf16[96,384]{1,0:T(8,128)(2,1)} async-done(((bf16[768,384]{1,0:T(8,128)(2,1)}), bf16[96,384]{1,0:T(8,128)(2,1)}) %reduce-scatter.9.cloned.1.call-update) | async-done | bytes 73744 | tf_op jit(solution)/shard_map/reduce_scatter | solution.py:537
  217.9 1.9 multiply_subtract_fusion.2
  219.7 36.3 %reduce-scatter.7.cloned.1.call-done = bf16[96,896]{1,0:T(8,128)(2,1)} async-done(((bf16[768,896]{1,0:T(8,128)(2,1)}), bf16[96,896]{1,0:T(8,128)(2,1)}) %reduce-scatter.7.cloned.1.call-update) | async-done | bytes 172048 | tf_op jit(solution)/shard_map/reduce_scatter | solution.py:607
  256.1 0.9 convert_element_type.106
  257.0 0.7 slice.226
  257.8 0.7 copy.188
  258.8 0.7 copy.189
  259.5 0.7 copy.190
  260.1 0.7 copy.191
  260.8 1.1 multiply_subtract_fusion.1
  261.9 0.6 copy.223
  (201 shorter events, 8.5 us)
Async XLA Ops:
  7.2 11.8 %copy-start.38 = (f32[96,6]{0,1:T(8,128)S(1)}, f32[96,6]{0,1:T(8,128)}, u32[]{:S(2)}) copy-start(f32[96,6]{0,1:T(8,128)} %param.35) | copy-start | bytes 6916
  7.2 12.6 %copy-start.47 = (f32[3,6]{1,0:T(4,128)S(1)}, f32[3,6]{1,0:T(4,128)}, u32[]{:S(2)}) copy-start(f32[3,6]{1,0:T(4,128)} %param.38) | copy-start | bytes 220
  7.2 13.8 %copy-start.48 = (f32[96,6]{0,1:T(8,128)S(1)}, f32[96,6]{0,1:T(8,128)}, u32[]{:S(2)}) copy-start(f32[96,6]{0,1:T(8,128)} %param.47) | copy-start | bytes 6916
  7.2 14.5 %copy-start.49 = (f32[96,6]{0,1:T(8,128)S(1)}, f32[96,6]{0,1:T(8,128)}, u32[]{:S(2)}) copy-start(f32[96,6]{0,1:T(8,128)} %param.46) | copy-start | bytes 6916
  7.3 15.2 %copy-start.41 = (f32[5,256]{1,0:T(8,128)S(1)}, f32[5,256]{1,0:T(8,128)}, u32[]{:S(2)}) copy-start(f32[5,256]{1,0:T(8,128)} %param.39) | copy-start | bytes 15364
  7.3 15.2 %copy-start.36 = (f32[6,384]{1,0:T(8,128)S(1)}, f32[6,384]{1,0:T(8,128)}, u32[]{:S(2)}) copy-start(f32[6,384]{1,0:T(8,128)} %param.37) | copy-start | bytes 27652
  7.3 15.3 %copy-start.11 = (bf16[1,512,768]{2,1,0:T(8,128)(2,1)S(1)}, bf16[1,512,768]{2,1,0:T(8,128)(2,1)}, u32[]{:S(2)}) copy-start(bf16[1,512,768]{2,1,0:T(8,128)(2,1)} %param.30) | copy-start | bytes 2359300
  7.3 46.0 %all-gather.6.cloned.1.call-start = ((), (), s32[]{:S(2)}) async-start(), calls=%async_computation.2 | async-start | bytes 2654208 | tf_op jit(solution)/shard_map/all_gather | solution.py:478
  18.2 0.7 copy-start.27
  19.0 35.6 %copy-start.39 = (f32[768]{0:T(1024)S(1)}, f32[768]{0:T(1024)}, u32[]{:S(2)}) copy-start(f32[768]{0:T(1024)} %param.32) | copy-start | bytes 9220
  19.0 178.6 %all-reduce.7.cloned.1.call-start = ((), (), s32[]{:S(2)}) async-start(), calls=%async_computation.3 | async-start | bytes 1572864 | tf_op jit(solution)/shard_map/psum | solution.py:536
  54.5 2.8 %copy-start.22 = (bf16[256,768]{1,0:T(8,128)(2,1)}, bf16[256,768]{1,0:T(8,128)(2,1)S(1)}, u32[]{:S(2)}) copy-start(bf16[256,768]{1,0:T(8,128)(2,1)S(1)} %reshape.244) | copy-start | bytes 1179652
  55.0 11.5 %copy-start.6 = (f32[512,256]{1,0:T(8,128)}, f32[512,256]{1,0:T(8,128)S(1)}, u32[]{:S(2)}) copy-start(f32[512,256]{1,0:T(8,128)S(1)} %fusion.42) | copy-start | bytes 1572868
  57.3 1.1 copy-start.20
  57.4 9.2 %copy-start.4 = (f32[512,384]{1,0:T(8,128)}, f32[512,384]{1,0:T(8,128)S(1)}, u32[]{:S(2)}) copy-start(f32[512,384]{1,0:T(8,128)S(1)} %slice.199) | copy-start | bytes 2359300
  58.4 8.0 %collective-permute-start = (f32[3,640]{1,0:T(4,128)S(1)}, f32[3,640]{1,0:T(4,128)S(1)}, u32[]{:S(2)}, u32[]{:S(2)}) collective-permute-start(f32[3,640]{1,0:T(4,128)S(1)} %fusion.86), channel_id=1, source_target_pairs={{0,16},{1,17},{2,18},{3,19},{4,20},{5,21},{6,22},{7,23},{8,24},{9,... | collective-permute-start | bytes 23048 | tf_op jit(solution)/shard_map/ppermute | solution.py:32
  61.1 2.3 copy-start.51
  66.5 1.9 copy-start.2
  77.3 2.2 copy-start.16
  77.3 2.2 copy-start.21
  79.5 2.9 %copy-start.17 = (f32[512,384]{1,0:T(8,128)}, f32[512,384]{1,0:T(8,128)S(1)}, u32[]{:S(2)}) copy-start(f32[512,384]{1,0:T(8,128)S(1)} %fusion.33) | copy-start | bytes 2359300
  82.4 10.6 %copy-start.8 = (f32[512,384]{1,0:T(8,128)}, f32[512,384]{1,0:T(8,128)S(1)}, u32[]{:S(2)}) copy-start(f32[512,384]{1,0:T(8,128)S(1)} %get-tuple-element.422) | copy-start | bytes 2359300
  90.2 2.8 %copy-start.18 = (f32[512,384]{1,0:T(8,128)S(1)}, f32[512,384]{1,0:T(8,128)}, u32[]{:S(2)}) copy-start(f32[512,384]{1,0:T(8,128)} %copy-done.17) | copy-start | bytes 2359300
  90.3 2.8 %copy-start.25 = (f32[512,384]{1,0:T(8,128)S(1)}, f32[512,384]{1,0:T(8,128)}, u32[]{:S(2)}) copy-start(f32[512,384]{1,0:T(8,128)} %get-tuple-element.448) | copy-start | bytes 2359300
  93.0 2.9 %copy-start.10 = (f32[512,384]{1,0:T(8,128)S(1)}, f32[512,384]{1,0:T(8,128)}, u32[]{:S(2)}) copy-start(f32[512,384]{1,0:T(8,128)} %fusion.77) | copy-start | bytes 2359300
  101.4 15.1 %copy-start.43 = (f32[384]{0:T(512)S(1)}, f32[384]{0:T(512)}, u32[]{:S(2)}) copy-start(f32[384]{0:T(512)} %mul.611) | copy-start | bytes 4612
  101.4 15.2 %copy-start.7 = (f32[512,256]{1,0:T(8,128)S(1)}, f32[512,256]{1,0:T(8,128)}, u32[]{:S(2)}) copy-start(f32[512,256]{1,0:T(8,128)} %copy-done.6) | copy-start | bytes 1572868
  101.4 15.2 %copy-start.15 = (f32[512,640]{1,0:T(8,128)S(1)}, f32[512,640]{1,0:T(8,128)}, u32[]{:S(2)}) copy-start(f32[512,640]{1,0:T(8,128)} %get-tuple-element.424) | copy-start | bytes 3932164
  116.4 2.8 %copy-start = (f32[3,512,4]{2,1,0:T(8,128)}, f32[3,512,4]{2,1,0:T(8,128)S(1)}, u32[]{:S(2)}) copy-start(f32[3,512,4]{2,1,0:T(8,128)S(1)} %get-tuple-element.179) | copy-start | bytes 73732
  116.4 1.6 copy-start.3
  116.4 1.8 copy-start.5
  118.3 4.6 %copy-start.9 = (f32[512,384]{1,0:T(8,128)S(1)}, f32[512,384]{1,0:T(8,128)}, u32[]{:S(2)}) copy-start(f32[512,384]{1,0:T(8,128)} %copy-done.8) | copy-start | bytes 2359300
  119.3 6.2 %copy-start.13 = (f32[512,640]{1,0:T(8,128)}, f32[512,640]{1,0:T(8,128)S(1)}, u32[]{:S(2)}) copy-start(f32[512,640]{1,0:T(8,128)S(1)} %get-tuple-element.421) | copy-start | bytes 3932164
  119.3 6.4 %copy-start.1 = (f32[3,512,4]{2,1,0:T(8,128)S(1)}, f32[3,512,4]{2,1,0:T(8,128)}, u32[]{:S(2)}) copy-start(f32[3,512,4]{2,1,0:T(8,128)} %copy-done) | copy-start | bytes 73732
  119.3 10.0 %collective-permute-start.1 = (f32[3,640]{1,0:T(4,128)S(1)}, f32[3,640]{1,0:T(4,128)S(1)}, u32[]{:S(2)}, u32[]{:S(2)}) collective-permute-start(f32[3,640]{1,0:T(4,128)S(1)} %slice.212), channel_id=1, source_target_pairs={{16,0},{17,1},{18,2},{19,3},{20,4},{21,5},{22,6},{23,7},{24,8},{25... | collective-permute-start | bytes 23048 | tf_op jit(solution)/shard_map/ppermute | solution.py:32
  125.5 92.4 %reduce-scatter.9.cloned.1.call-start = ((), (), s32[]{:S(2)}) async-start(), calls=%async_computation.5 | async-start | bytes 663552 | tf_op jit(solution)/shard_map/reduce_scatter | solution.py:537
  126.0 1.1 copy-start.19
  126.1 2.2 copy-start.50
  126.1 2.2 copy-start.52
  126.4 2.4 copy-start.12
  128.2 1.3 copy-start.14
  129.1 126.9 %reduce-scatter.7.cloned.1.call-start = ((), (), s32[]{:S(2)}) async-start(), calls=%async_computation.4 | async-start | bytes 1548288 | tf_op jit(solution)/shard_map/reduce_scatter | solution.py:607
  129.3 1.6 copy-start.28
  130.1 0.7 copy-start.29
  131.9 1.6 copy-start.23
  176.3 17.2 %copy-start.45 = (f32[5,256]{1,0:T(8,128)S(1)}, f32[5,256]{1,0:T(8,128)}, u32[]{:S(2)}) copy-start(f32[5,256]{1,0:T(8,128)} %param.54) | copy-start | bytes 15364
  176.3 18.5 %copy-start.44 = (f32[6,384]{1,0:T(8,128)S(1)}, f32[6,384]{1,0:T(8,128)}, u32[]{:S(2)}) copy-start(f32[6,384]{1,0:T(8,128)} %param.50) | copy-start | bytes 27652
  176.3 19.8 %copy-start.35 = (f32[192,32]{0,1:T(8,128)S(1)}, f32[192,32]{0,1:T(8,128)}, u32[]{:S(2)}) copy-start(f32[192,32]{0,1:T(8,128)} %param.34) | copy-start | bytes 73732
  176.3 19.8 %copy-start.40 = (f32[192,32]{0,1:T(8,128)S(1)}, f32[192,32]{0,1:T(8,128)}, u32[]{:S(2)}) copy-start(f32[192,32]{0,1:T(8,128)} %param.44) | copy-start | bytes 73732
  190.7 10.3 %copy-start.37 = (f32[6,384]{1,0:T(8,128)}, f32[6,384]{1,0:T(8,128)S(1)}, u32[]{:S(2)}) copy-start(f32[6,384]{1,0:T(8,128)S(1)} %reshape.256) | copy-start | bytes 27652
  190.8 6.7 %copy-start.46 = (f32[3,6]{1,0:T(4,128)}, f32[3,6]{1,0:T(4,128)S(1)}, u32[]{:S(2)}) copy-start(f32[3,6]{1,0:T(4,128)S(1)} %reshape.258) | copy-start | bytes 220
  190.8 6.7 %copy-start.42 = (f32[5,256]{1,0:T(8,128)}, f32[5,256]{1,0:T(8,128)S(1)}, u32[]{:S(2)}) copy-start(f32[5,256]{1,0:T(8,128)S(1)} %reshape.259) | copy-start | bytes 15364
  197.6 20.3 %copy-start.26 = (f32[384,96]{0,1:T(8,128)S(1)}, f32[384,96]{0,1:T(8,128)}, u32[]{:S(2)}) copy-start(f32[384,96]{0,1:T(8,128)} %param.36) | copy-start | bytes 442372
  201.1 57.4 %copy-start.33 = (f32[96,6]{1,0:T(8,128)S(1)}, f32[96,6]{1,0:T(8,128)}, u32[]{:S(2)}) copy-start(f32[96,6]{1,0:T(8,128)} %copy.181) | copy-start | bytes 6916
  201.1 57.4 %copy-start.34 = (f32[96,6]{1,0:T(8,128)S(1)}, f32[96,6]{1,0:T(8,128)}, u32[]{:S(2)}) copy-start(f32[96,6]{1,0:T(8,128)} %copy.179) | copy-start | bytes 6916
  201.1 57.7 %copy-start.32 = (f32[96,6]{1,0:T(8,128)S(1)}, f32[96,6]{1,0:T(8,128)}, u32[]{:S(2)}) copy-start(f32[96,6]{1,0:T(8,128)} %copy.186) | copy-start | bytes 6916
  201.1 59.7 %copy-start.24 = (f32[2,96,384]{2,1,0:T(8,128)S(1)}, f32[2,96,384]{2,1,0:T(8,128)}, u32[]{:S(2)}) copy-start(f32[2,96,384]{2,1,0:T(8,128)} %param.33) | copy-start | bytes 884740
  201.1 59.7 %copy-start.30 = (f32[2,96,384]{2,1,0:T(8,128)S(1)}, f32[2,96,384]{2,1,0:T(8,128)}, u32[]{:S(2)}) copy-start(f32[2,96,384]{2,1,0:T(8,128)} %param.42) | copy-start | bytes 884740
  201.1 59.7 %copy-start.31 = (f32[2,96,384]{2,1,0:T(8,128)S(1)}, f32[2,96,384]{2,1,0:T(8,128)}, u32[]{:S(2)}) copy-start(f32[2,96,384]{2,1,0:T(8,128)} %param.43) | copy-start | bytes 884740
Sparse Core Ops, SparseCore 0:
  19.1 34.1 all-gather.5
  125.6 56.1 all-reduce.6
  184.0 33.7 reduce-scatter.8
  220.0 35.9 reduce-scatter.6
